TPU v7x, 128 devices: a whole 4x4x4 slice. The times are simulated.
128 devices in a mesh: energy: 8 (over z, core), cuts: 16 (over y, x).
Axes of the slice: x: 4, y: 4, z: 4, core: 2. Of those that a mesh axis runs over, the one named last changes fastest.
Arguments:
- coupling: bfloat16 [16, 720, 720], P('cuts'), may hold values from -0.3125 to 0.3125
- block_mask: int32 [16, 6, 6], P('cuts'), may hold values from 0 to 1, as said below
- levels: float32 [16, 720], P('cuts'), may hold values from -4 to 4
- dwell: float32 [16, 720], P('cuts'), may hold values from 0.5 to 3
- polarization: bfloat16 [2, 16, 16, 720, 720], P(None, 'energy', 'cuts'), may hold values from -6 to 6
Outputs:
- sigma: bfloat16 [2, 16, 16, 720, 720], P(None, 'energy', 'cuts')
Inputs may be any that keep to these rules, and one draw needn't show every extreme that they name: `block_mask`: 1 where a coupling block of a slice is present, else 0; the diagonal blocks are always present.
All inputs are finite; a program needn't handle non-finite values.
Results may differ from a plain program's by a relative error of at most 0.023.
Values may be sent and summed in bfloat16 or wider, within the bound.
A program may use at most 192 MiB of HBM per device.

v0:
```python
import functools
import math

import jax
import jax.numpy as jnp
from jax import lax
from jax.experimental import pallas as pl
from jax.experimental.pallas import tpu as pltpu
from jax.sharding import PartitionSpec as P

MESH = pl.DeviceIdType.MESH
F32 = jnp.float32
BF16 = jnp.bfloat16

NX = 4
NY = 4
NG = 8
NI = NX * NY
ROWS = 96
CH = 16
H0 = 320
SPREAD = (0, 2)
GA = 64
EB = 8
EC = 16


def row_start(g, n):
    return jnp.minimum(g * ROWS, n - ROWS)


def pairwise(parts, value):
    rank = 0
    while parts and parts[-1][0] == rank:
        value = parts.pop()[1] + value
        rank += 1
    parts.append((rank, value))


def collect(parts):
    total = parts.pop()[1]
    while parts:
        total = parts.pop()[1] + total
    return total


def kernel(
    coup, mask, lev, dwl, pol, out,
    call, lall, dall, tab, rph, x, p, sig,
    a_send, a_recv, b_send, b_recv, f_send, c_send, c_recv, l_send, l_recv,
    p_send, p_recv, o_send, o_recv, loc,
):
    n = coup.shape[1]
    ne = x.shape[0]
    nch = ROWS // CH
    g = lax.axis_index("energy")
    i = lax.axis_index("cuts")
    core = g % 2
    yy = i // NX
    xx = i % NX
    r0 = pl.multiple_of(row_start(g, n), 16)

    barrier = pltpu.get_barrier_semaphore()
    for d in range(1, NG):
        pl.semaphore_signal(barrier, 1, device_id=((g + d) % NG, i), device_id_type=MESH)
    for d in range(1, NI):
        pl.semaphore_signal(barrier, 1, device_id=(g, (i + d) % NI), device_id_type=MESH)

    nb = mask.shape[0]
    bw = n // nb
    left = (
        lax.broadcasted_iota(jnp.int32, (n, nb), 0) // bw
        == lax.broadcasted_iota(jnp.int32, (n, nb), 1)
    ).astype(F32).astype(BF16)
    right = (
        lax.broadcasted_iota(jnp.int32, (nb, n), 1) // bw
        == lax.broadcasted_iota(jnp.int32, (nb, n), 0)
    ).astype(F32).astype(BF16)
    small = mask[:, 0, :].astype(F32).astype(BF16)
    wide = jnp.dot(small, right, preferred_element_type=F32).astype(BF16)
    spread = jnp.dot(left, wide, preferred_element_type=F32)
    call[i] = (coup[0].astype(F32) * spread).astype(BF16)

    pl.semaphore_wait(barrier, NG - 1 + NI - 1)

    def share_rows(k):
        return pl.ds(0, H0) if k == 0 else pl.ds(H0, n - H0)

    class Share:
        def __init__(self, make, other=False):
            self.make = make
            self.other = other

        def each(self, act):
            for k in range(2):
                rows = share_rows(1 - k if self.other else k)
                pl.when(core == k)(functools.partial(act, rows))

        def start(self):
            self.each(lambda rows: self.make(rows).start())

        def wait(self):
            self.each(lambda rows: self.make(rows).wait())

        def wait_send(self):
            self.each(lambda rows: self.make(rows).wait_send())

    def send_half(j, dest, ssem, rsem):
        return Share(
            lambda rows: pltpu.make_async_remote_copy(
                call.at[j, rows, :], call.at[j, rows, :], ssem, rsem,
                device_id=(g, dest), device_id_type=MESH,
            )
        )

    def arrived(j, sem, other=False):
        Share(
            lambda rows: pltpu.make_async_copy(
                call.at[j, rows, :], call.at[j, rows, :], sem
            ),
            other,
        ).wait()

    def l_copy(src, dst, k, dest):
        return pltpu.make_async_remote_copy(
            src, dst.at[i], l_send.at[k, dest], l_recv.at[k, i],
            device_id=(g, dest), device_id_type=MESH,
        )

    def l_start(d, _):
        dest = (i + d) % NI
        l_copy(lev, lall, 0, dest).start()
        l_copy(dwl, dall, 1, dest).start()
        return 0

    lax.fori_loop(1, NI, l_start, 0)

    relays = jnp.logical_and(core == 0, yy < NY - 1)

    def row_mate(d):
        return yy * NX + (xx + d) % NX

    for d in (1, 3, 2):
        ok = jnp.logical_or(relays, xx + d < NX)

        @pl.when(ok)
        def _():
            send_half(i, row_mate(d), a_send.at[0, d], a_recv.at[i]).start()

    def column_send(d):
        send_half(i, i + d * NX, a_send.at[1, d], a_recv.at[i]).start()

    for d in (1, 3):
        pl.when(yy + d < NY)(functools.partial(column_send, d))
    pl.when(jnp.logical_and(core == 1, yy + 2 < NY))(functools.partial(column_send, 2))

    def p_copy(d):
        dest = (g + d) % NG
        rd = pl.multiple_of(row_start(dest, n), 16)
        return pltpu.make_async_remote_copy(
            pol.at[:, :, 0, pl.ds(rd, ROWS), :], p.at[:, pl.ds(2 * g, 2)],
            p_send.at[d], p_recv.at[g], device_id=(dest, i), device_id_type=MESH,
        )

    for d in range(1, NG):
        p_copy(d).start()
    p_own = pltpu.make_async_copy(
        pol.at[:, :, 0, pl.ds(r0, ROWS), :], p.at[:, pl.ds(2 * g, 2)], p_recv.at[g]
    )
    p_own.start()

    lall[i] = lev[...]
    dall[i] = dwl[...]

    def l_wait(d, _):
        src = (i + d) % NI
        pltpu.make_async_copy(lall.at[src], lall.at[src], l_recv.at[0, src]).wait()
        pltpu.make_async_copy(dall.at[src], dall.at[src], l_recv.at[1, src]).wait()
        return 0

    lax.fori_loop(1, NI, l_wait, 0)

    tab[0, 0] = jnp.ones((ne, n), F32)
    tab[0, 1] = jnp.zeros((ne, n), F32)
    energy = lax.broadcasted_iota(jnp.int32, (ne, n), 0).astype(F32)

    def tables(j, _):
        phase = (energy - lall[j]) * dall[j]
        tab[j + 1, 0] = jnp.cos(phase)
        tab[j + 1, 1] = jnp.sin(phase)
        return 0

    lax.fori_loop(0, i, tables, 0)

    def share(j):
        return Share(
            lambda rows: pltpu.make_async_remote_copy(
                call.at[j, rows, :], call.at[j, rows, :], c_send.at[j], c_recv.at[j],
                device_id=(g + 1 - 2 * core, i), device_id_type=MESH,
            )
        )

    def own_line(j):
        return jnp.where(core == 0, j // NX == yy, j % NX == xx)

    def relay(j, dest):
        return send_half(j, dest, f_send.at[j], b_recv.at[j])

    @pl.when(core == 0)
    def _():
        @pl.when(yy == 1)
        def _():
            send_half(i, i - NX, a_send.at[1, 2], b_recv.at[i]).start()

        for d in (1, 3):
            j = yy * NX + (xx + NX - d) % NX

            @pl.when(jnp.logical_or(relays, j < i))
            def _():
                arrived(j, a_recv.at[j])

            @pl.when(j < i)
            def _():
                share(j).start()

            for k in (1, 3):

                @pl.when(yy + k < NY)
                def _():
                    send_half(j, i + k * NX, b_send.at[d, k], b_recv.at[j]).start()

            if d == 1:

                @pl.when(yy == 1)
                def _():
                    send_half(j, i - NX, b_send.at[d, 2], b_recv.at[j]).start()

        @pl.when(yy == 0)
        def _():
            for d in (0, 1):
                j = NX + (xx + NX - d) % NX
                arrived(j, b_recv.at[j])
                relay(j, i + 3 * NX).start()

    def spread_row(d):
        @pl.when(jnp.logical_and(core == 1, yy >= d))
        def _():
            j = i - d * NX
            arrived(j, a_recv.at[j])
            share(j).start()
            for k in (1, 3, 2):
                send_half(j, row_mate(k), b_send.at[d, k], b_recv.at[j]).start()

    spread_row(1)

    pick = (
        lax.broadcasted_iota(jnp.int32, (ROWS, n), 1)
        == lax.broadcasted_iota(jnp.int32, (ROWS, n), 0) + r0
    )
    col_lev = jnp.sum(jnp.where(pick, lev[...], 0.0), axis=1, keepdims=True)
    col_dwl = jnp.sum(jnp.where(pick, dwl[...], 0.0), axis=1, keepdims=True)
    col_phase = (
        lax.broadcasted_iota(jnp.int32, (ROWS, ne), 1).astype(F32) - col_lev
    ) * col_dwl
    rph[0] = jnp.cos(col_phase)
    rph[1] = jnp.sin(col_phase)

    def init(e, _):
        lane = lax.broadcasted_iota(jnp.int32, (ROWS, ne), 1) == e
        rc = jnp.sum(jnp.where(lane, rph[0], 0.0), axis=1, keepdims=True)
        rs = jnp.sum(jnp.where(lane, rph[1], 0.0), axis=1, keepdims=True)
        c = tab[i, 0, pl.ds(e, 1), :]
        s = tab[i, 1, pl.ds(e, 1), :]
        base = call[i, pl.ds(r0, ROWS), :].astype(F32) * math.sqrt(n / ne)
        x[e, 0] = (base * (rc * c - rs * s)).astype(BF16)
        x[e, 1] = (-base * (rc * s + rs * c)).astype(BF16)
        return 0

    lax.fori_loop(0, ne, init, 0)

    def late():
        j = yy * NX + (xx + 2) % NX

        @pl.when(jnp.logical_or(relays, j < i))
        def _():
            arrived(j, a_recv.at[j])

        @pl.when(j < i)
        def _():
            share(j).start()

        for k in (1, 3):

            @pl.when(yy + k < NY)
            def _():
                send_half(j, i + k * NX, b_send.at[2, k], b_recv.at[j]).start()

    def passes(j):
        first = jnp.logical_and(yy == 1, j // NX == 0)
        second = jnp.logical_and(yy == 2, jnp.logical_and(j // NX == 1, (xx + NX - j % NX) % NX >= 2))
        return jnp.logical_and(core == 0, jnp.logical_or(first, second))

    def take(j):
        @pl.when(jnp.logical_not(own_line(j)))
        def _():
            direct = jnp.where(
                core == 0,
                jnp.logical_and(j % NX == xx, yy - j // NX != 2),
                j // NX == yy,
            )

            @pl.when(direct)
            def _():
                arrived(j, a_recv.at[j])

            @pl.when(jnp.logical_not(direct))
            def _():
                arrived(j, b_recv.at[j])

            @pl.when(passes(j))
            def _():
                relay(j, i + NX).start()

            share(j).start()

    @pl.when(jnp.logical_and(core == 0, i == 0))
    def _():
        late()

    @pl.when(i > 0)
    def _():
        take(i - 1)


    def block(j, b, rows, count):
        first, size = rows
        z = x[pl.ds(b * count, count), :, first : first + size, :]
        z = z.reshape(count * 2 * size, n)
        r = jnp.dot(z, call[j], preferred_element_type=F32)
        for k in range(count):
            e = b * count + k
            c = tab[j, 0, pl.ds(e, 1), :]
            s = tab[j, 1, pl.ds(e, 1), :]
            re = r[2 * k * size : (2 * k + 1) * size]
            im = r[(2 * k + 1) * size : (2 * k + 2) * size]
            x[e, 0, first : first + size, :] = (re * c + im * s).astype(BF16)
            x[e, 1, first : first + size, :] = (im * c - re * s).astype(BF16)

    def chain(q, _):
        j = i - 1 - q
        arrived(j, c_recv.at[j], other=True)

        def part(b, _):
            block(j, b, (0, GA), EB)

            @pl.when(b == 0)
            def _():
                @pl.when(jnp.logical_and(core == 0, q == 0))
                def _():
                    late()

                for d in range(2, NY):
                    pl.when(q == SPREAD[d - 2])(functools.partial(spread_row, d))

                @pl.when(j > 0)
                def _():
                    take(j - 1)

            return 0

        lax.fori_loop(0, ne // EB, part, 0)
        return 0

    lax.fori_loop(0, i, chain, 0)

    def chain_rest(q, _):
        j = i - 1 - q

        def part(b, _):
            block(j, b, (GA, ROWS - GA), EC)
            return 0

        lax.fori_loop(0, ne // EC, part, 0)
        return 0

    p_own.wait()
    for d in range(1, NG):
        src = (g + NG - d) % NG
        view = p.at[:, pl.ds(2 * src, 2)]
        pltpu.make_async_copy(view, view, p_recv.at[src]).wait()

    def o_copy(d, q):
        dest = (g + d) % NG
        rows = pl.ds(pl.multiple_of(r0 + q * CH, CH), CH)
        return pltpu.make_async_remote_copy(
            sig.at[:, pl.ds(2 * dest, 2), pl.ds(pl.multiple_of(q * CH, CH), CH), :],
            out.at[:, :, 0, rows, :],
            o_send.at[d, q], o_recv.at[g, q], device_id=(dest, i), device_id_type=MESH,
        )

    def o_own(q):
        rows = pl.ds(pl.multiple_of(r0 + q * CH, CH), CH)
        return pltpu.make_async_copy(
            sig.at[:, pl.ds(2 * g, 2), pl.ds(pl.multiple_of(q * CH, CH), CH), :],
            out.at[:, :, 0, rows, :], loc.at[q],
        )

    q_first = (g * ROWS - r0) // CH

    def chunk(q, _):
        rows = pl.ds(pl.multiple_of(q * CH, CH), CH)

        def tile(lane):
            ga = [x[e, 0, rows, lane] for e in range(ne)]
            gb = [x[e, 1, rows, lane] for e in range(ne)]
            for e in range(ne):
                res, ims = [], []
                for w in range(e + 1):
                    pr = p[0, w, rows, lane]
                    pi = p[1, w, rows, lane]
                    pairwise(res, pr * ga[e - w] - pi * gb[e - w])
                    pairwise(ims, pr * gb[e - w] + pi * ga[e - w])
                sig[0, e, rows, lane] = collect(res)
                sig[1, e, rows, lane] = collect(ims)

        def whole(t, _):
            tile(pl.ds(pl.multiple_of(t * 128, 128), 128))
            return 0

        lax.fori_loop(0, n // 128, whole, 0)
        if n % 128:
            tile(pl.ds(n - n % 128, n % 128))
        for d in range(1, NG):
            o_copy(d, q).start()
        o_own(q).start()
        return 0

    lax.fori_loop(q_first, GA // CH, chunk, 0)
    lax.fori_loop(0, i, chain_rest, 0)
    lax.fori_loop(GA // CH, nch, chunk, 0)

    for d in range(1, NX):
        ok = jnp.logical_or(relays, xx + d < NX)

        @pl.when(ok)
        def _():
            send_half(i, row_mate(d), a_send.at[0, d], a_recv.at[i]).wait_send()

    def sent(sem):
        send_half(i, i, sem, a_recv.at[i]).wait_send()

    for d in (1, 3):
        pl.when(yy + d < NY)(functools.partial(sent, a_send.at[1, d]))
    ok = jnp.where(core == 1, yy + 2 < NY, yy == 1)
    pl.when(ok)(functools.partial(sent, a_send.at[1, 2]))
    for d in range(1, NX):
        for k in (1, 3):
            ok = jnp.where(core == 0, yy + k < NY, yy >= d)
            pl.when(ok)(functools.partial(sent, b_send.at[d, k]))
        ok = jnp.where(core == 0, yy == 1 if d == 1 else False, yy >= d)
        pl.when(ok)(functools.partial(sent, b_send.at[d, 2]))

    @pl.when(core == 0)
    def _():
        for d in range(NX):
            j = (xx + NX - d) % NX
            pl.when(yy == 1)(functools.partial(sent, f_send.at[j]))
            pl.when(yy == (0 if d < 2 else 2))(functools.partial(sent, f_send.at[NX + j]))

    def share_done(j, _):
        share(j).wait_send()
        return 0

    lax.fori_loop(0, i, share_done, 0)

    def l_done(d, _):
        dest = (i + d) % NI
        l_copy(lev, lall, 0, dest).wait_send()
        l_copy(dwl, dall, 1, dest).wait_send()
        return 0

    lax.fori_loop(1, NI, l_done, 0)
    for d in range(1, NG):
        p_copy(d).wait_send()

    def o_done(q, _):
        for d in range(1, NG):
            o_copy(d, q).wait_send()
        o_own(q).wait()
        return 0

    lax.fori_loop(q_first, nch, o_done, 0)
    for d in range(1, NG):
        src = (g + d) % NG
        rs = row_start(src, n)
        qs = (src * ROWS - rs) // CH

        def o_wait(q, _):
            view = out.at[:, :, 0, pl.ds(pl.multiple_of(rs + q * CH, CH), CH), :]
            pltpu.make_async_copy(view, view, o_recv.at[src, q]).wait()
            return 0

        lax.fori_loop(qs, nch, o_wait, 0)


def shards(coupling, block_mask, levels, dwell, polarization):
    n = levels.shape[1]
    ne = 2 * NG
    vmem = pl.BlockSpec(memory_space=pltpu.VMEM)
    anyw = pl.BlockSpec(memory_space=pl.ANY)
    dma = pltpu.SemaphoreType.DMA
    return pl.pallas_call(
        kernel,
        out_shape=jax.ShapeDtypeStruct(polarization.shape, BF16),
        in_specs=[vmem, vmem, vmem, vmem, anyw],
        out_specs=anyw,
        scratch_shapes=[
            pltpu.VMEM((NI, n, n), BF16),
            pltpu.VMEM((NI, 1, n), F32),
            pltpu.VMEM((NI, 1, n), F32),
            pltpu.VMEM((NI + 1, 2, ne, n), F32),
            pltpu.VMEM((2, ROWS, ne), F32),
            pltpu.VMEM((ne, 2, ROWS, n), BF16),
            pltpu.VMEM((2, ne, ROWS, n), BF16),
            pltpu.VMEM((2, ne, ROWS, n), BF16),
            dma((2, NX)), dma((NI,)),
            dma((NX, NY)), dma((NI,)), dma((NI,)),
            dma((NI,)), dma((NI,)),
            dma((2, NI)), dma((2, NI)),
            dma((NG,)), dma((NG,)),
            dma((NG, ROWS // CH)), dma((NG, ROWS // CH)),
            dma((ROWS // CH,)),
        ],
        compiler_params=pltpu.CompilerParams(
            collective_id=0, has_side_effects=True, vmem_limit_bytes=62 * 1024 * 1024
        ),
        name="gw_sigma",
    )(coupling, jnp.transpose(block_mask, (1, 0, 2)), levels, dwell, polarization)


def solution(mesh):
    return jax.shard_map(
        shards,
        mesh=mesh,
        in_specs=(
            P("cuts", None, None),
            P("cuts", None, None),
            P("cuts", None),
            P("cuts", None),
            P(None, "energy", "cuts", None, None),
        ),
        out_specs=P(None, "energy", "cuts", None, None),
        check_vma=False,
    )
```

profile of v0, /device:TPU:31, one launch (start us, length us, event | category | flops | bytes accessed | tf_op | source)
XLA Modules:
  0.0 152.2 jit_solution(16993203951989493072)
XLA Ops:
  0.0 147.6 %gw_sigma.1 = bf16[2,2,1,720,720]{4,3,2,1,0:T(8,128)(2,1)} custom-call(bf16[1,720,720]{2,1,0:T(8,128)(2,1)} %coup.1, s32[6,1,6]{2,1,0:T(1,128)} %bitcast.1, f32[1,720]{1,0:T(1,128)} %lev.1, f32[1,720]{1,0:T(1,128)} %dwl.1, bf16[2,2,1,720,720]{4,3,2,1,0:T(8,128)(2,1)} %pol.1), custom_call_target="tpu_custom_call" | custom-call | tf_op jit(solution)/shard_map/gw_sigma/pallas_call | solution.py:512
  147.6 4.6 %copy.7 = bf16[2,2,1,720,720]{4,3,2,1,0:T(8,128)(2,1)} copy(bf16[2,2,1,720,720]{4,3,2,1,0:T(8,128)(2,1)} %gw_sigma.1) | data formatting | bytes 8294400
where the time goes:
time: 152 us
  Pallas kernels  148 us (97%)
  local copies, waits for them, and re-layouts  4.63 us (3%)
    pallas_call x1, Pallas kernels, shards(): pl.pallas_call(kernel, out_shape=jax.ShapeDtypeStruct(polarization.shape,...  148 us
    unnamed x1, local copies, waits for them, and re-layouts  4.63 us

commit v1 on v0

--- a/solution.py
+++ b/solution.py
@@ -201,7 +201,9 @@
         )
 
     def own_line(j):
-        return jnp.where(core == 0, j // NX == yy, j % NX == xx)
+        return jnp.where(
+            core == 0, jnp.logical_and(relays, j // NX == yy), j % NX == xx
+        )
 
     def relay(j, dest):
         return send_half(j, dest, f_send.at[j], b_recv.at[j])
@@ -212,28 +214,28 @@
         def _():
             send_half(i, i - NX, a_send.at[1, 2], b_recv.at[i]).start()
 
-        for d in (1, 3):
-            j = yy * NX + (xx + NX - d) % NX
-
-            @pl.when(jnp.logical_or(relays, j < i))
-            def _():
+        @pl.when(relays)
+        def _():
+            for d in (1, 3):
+                j = yy * NX + (xx + NX - d) % NX
+
                 arrived(j, a_recv.at[j])
 
-            @pl.when(j < i)
-            def _():
-                share(j).start()
-
-            for k in (1, 3):
-
-                @pl.when(yy + k < NY)
+                @pl.when(j < i)
                 def _():
-                    send_half(j, i + k * NX, b_send.at[d, k], b_recv.at[j]).start()
-
-            if d == 1:
-
-                @pl.when(yy == 1)
-                def _():
-                    send_half(j, i - NX, b_send.at[d, 2], b_recv.at[j]).start()
+                    share(j).start()
+
+                for k in (1, 3):
+
+                    @pl.when(yy + k < NY)
+                    def _():
+                        send_half(j, i + k * NX, b_send.at[d, k], b_recv.at[j]).start()
+
+                if d == 1:
+
+                    @pl.when(yy == 1)
+                    def _():
+                        send_half(j, i - NX, b_send.at[d, 2], b_recv.at[j]).start()
 
         @pl.when(yy == 0)
         def _():
@@ -281,9 +283,7 @@
     def late():
         j = yy * NX + (xx + 2) % NX
 
-        @pl.when(jnp.logical_or(relays, j < i))
-        def _():
-            arrived(j, a_recv.at[j])
+        arrived(j, a_recv.at[j])
 
         @pl.when(j < i)
         def _():
@@ -305,7 +305,10 @@
         def _():
             direct = jnp.where(
                 core == 0,
-                jnp.logical_and(j % NX == xx, yy - j // NX != 2),
+                jnp.logical_or(
+                    j // NX == yy,
+                    jnp.logical_and(j % NX == xx, yy - j // NX != 2),
+                ),
                 j // NX == yy,
             )
 
@@ -355,7 +358,7 @@
 
             @pl.when(b == 0)
             def _():
-                @pl.when(jnp.logical_and(core == 0, q == 0))
+                @pl.when(jnp.logical_and(relays, q == 0))
                 def _():
                     late()
 

time: 152 us -> 146 us (0.961)
  Pallas kernels: 148 us -> 141 us
    pallas_call x1, Pallas kernels: 148 us -> 141 us  [shards(): pl.pallas_call(kernel, out_shape=jax.ShapeDtypeStruct(polarization.shape,...]
where the time goes in v1:
time: 146 us
  Pallas kernels  141 us (97%)
  local copies, waits for them, and re-layouts  4.63 us (3%)
    pallas_call x1, Pallas kernels, shards(): pl.pallas_call(kernel, out_shape=jax.ShapeDtypeStruct(polarization.shape,...  141 us
    unnamed x1, local copies, waits for them, and re-layouts  4.63 us

profile of v1, /device:TPU:31, one launch (start us, length us, event | category | flops | bytes accessed | tf_op | source)
XLA Modules:
  0.0 145.6 jit_solution(7340035194803091585)
XLA Ops:
  0.0 141.0 %gw_sigma.1 = bf16[2,2,1,720,720]{4,3,2,1,0:T(8,128)(2,1)} custom-call(bf16[1,720,720]{2,1,0:T(8,128)(2,1)} %coup.1, s32[6,1,6]{2,1,0:T(1,128)} %bitcast.1, f32[1,720]{1,0:T(1,128)} %lev.1, f32[1,720]{1,0:T(1,128)} %dwl.1, bf16[2,2,1,720,720]{4,3,2,1,0:T(8,128)(2,1)} %pol.1), custom_call_target="tpu_custom_call" | custom-call | tf_op jit(solution)/shard_map/gw_sigma/pallas_call | solution.py:515
  141.0 4.6 %copy.7 = bf16[2,2,1,720,720]{4,3,2,1,0:T(8,128)(2,1)} copy(bf16[2,2,1,720,720]{4,3,2,1,0:T(8,128)(2,1)} %gw_sigma.1) | data formatting | bytes 8294400

commit v2 on v1

--- a/solution.py
+++ b/solution.py
@@ -225,11 +225,7 @@
                 def _():
                     share(j).start()
 
-                for k in (1, 3):
-
-                    @pl.when(yy + k < NY)
-                    def _():
-                        send_half(j, i + k * NX, b_send.at[d, k], b_recv.at[j]).start()
+                send_half(j, i + NX, b_send.at[d, 1], b_recv.at[j]).start()
 
                 if d == 1:
 
@@ -243,6 +239,10 @@
                 j = NX + (xx + NX - d) % NX
                 arrived(j, b_recv.at[j])
                 relay(j, i + 3 * NX).start()
+
+            for d in (1, 3):
+                j = (xx + NX - d) % NX
+                send_half(j, i + 3 * NX, b_send.at[d, 3], b_recv.at[j]).start()
 
     def spread_row(d):
         @pl.when(jnp.logical_and(core == 1, yy >= d))
@@ -515,7 +515,7 @@
     return pl.pallas_call(
         kernel,
         out_shape=jax.ShapeDtypeStruct(polarization.shape, BF16),
-        in_specs=[vmem, vmem, vmem, vmem, anyw],
+        in_specs=[vmem, vmem, vmem, vmem, pl.BlockSpec(memory_space=pltpu.HBM)],
         out_specs=anyw,
         scratch_shapes=[
             pltpu.VMEM((NI, n, n), BF16),
@@ -535,7 +535,7 @@
             dma((ROWS // CH,)),
         ],
         compiler_params=pltpu.CompilerParams(
-            collective_id=0, has_side_effects=True, vmem_limit_bytes=62 * 1024 * 1024
+            collective_id=0, has_side_effects=True, vmem_limit_bytes=48 * 1024 * 1024
         ),
         name="gw_sigma",
     )(coupling, jnp.transpose(block_mask, (1, 0, 2)), levels, dwell, polarization)

time: 146 us -> 146 us (level)
    pallas_call x1, Pallas kernels: 141 us -> 140 us  [shards(): pl.pallas_call(kernel, out_shape=jax.ShapeDtypeStruct(polarization.shape,...]
    unnamed x1 -> x9, local copies, waits for them, and re-layouts: 4.63 us -> 5.39 us
where the time goes in v2:
time: 146 us; the launch traced here: 145 us
  Pallas kernels  140 us (96%)
  local copies, waits for them, and re-layouts  5.39 us (4%)
    pallas_call x1, Pallas kernels, shards(): pl.pallas_call(kernel, out_shape=jax.ShapeDtypeStruct(polarization.shape,...  140 us
    unnamed x9, local copies, waits for them, and re-layouts  5.39 us

profile of v2, /device:TPU:31, one launch (start us, length us, event | category | flops | bytes accessed | tf_op | source)
XLA Modules:
  0.0 144.9 jit_solution(11717798251070764572)
XLA Ops:
  0.0 0.0 copy-start
  0.0 1.2 copy-done
  1.2 0.0 copy-start.1
  1.2 0.7 copy-done.1
  1.9 0.0 copy-start.2
  1.9 0.7 copy-done.2
  2.6 0.0 copy-start.3
  2.6 0.7 copy-done.3
  3.3 139.5 %gw_sigma.1 = bf16[2,2,1,720,720]{4,3,2,1,0:T(8,128)(2,1)S(1)} custom-call(bf16[1,720,720]{2,1,0:T(8,128)(2,1)S(1)} %copy-done, s32[6,1,6]{2,1,0:T(1,128)S(1)} %bitcast.1, f32[1,720]{1,0:T(1,128)S(1)} %copy-done.2, f32[1,720]{1,0:T(1,128)S(1)} %copy-done.3, bf16[2,2,1,720,720]{4,3,2,1,0:T(8,128)(2,1)} %pol.1), custom_call_target="tpu_custom_call" | custom-call | tf_op jit(solution)/shard_map/gw_sigma/pallas_call | solution.py:515
  142.8 2.1 %copy.7 = bf16[2,2,1,720,720]{4,3,2,1,0:T(8,128)(2,1)} copy(bf16[2,2,1,720,720]{4,3,2,1,0:T(8,128)(2,1)S(1)} %gw_sigma.1) | data formatting | bytes 8294400
Async XLA Ops:
  0.0 1.2 copy-start
  1.2 0.7 copy-start.1
  1.9 0.7 copy-start.2
  2.6 0.7 copy-start.3
